TPU v7x, 256 devices: a whole 4x4x8 slice. The times are simulated.
256 devices in a mesh: row: 32 (over y, z), col: 8 (over x, core).
Axes of the slice: x: 4, y: 4, z: 8, core: 2. Of those that a mesh axis runs over, the one named last changes fastest.
Arguments:
- panel: float32 [8, 32, 256, 256], P(None, 'row', None, 'col'), may hold values from -0.1875 to 0.1875
- slab: bfloat16 [8, 32, 256, 4, 8, 256], P(None, 'row', None, None, 'col'), may hold values from -6 to 6
- cotangent: bfloat16 [8, 32, 256, 4, 8, 256], P(None, 'row', None, None, 'col'), may hold values from -0.0625 to 0.0625
- inverse: float32 [256, 256], replicated, may hold values from -2 to 8, as said below
Outputs:
- updated: bfloat16 [8, 32, 256, 4, 8, 256], P(None, 'row', None, None, 'col')
- grad_panel: float32 [8, 32, 256, 256], P(None, 'row', None, 'col')
- grad_inverse: float32 [256, 256], P(None, 'col')
Inputs may be any that keep to these rules, and one draw needn't show every extreme that they name: `inverse`: lower triangular; diagonal entries between 4 and 8.
All inputs are finite; a program needn't handle non-finite values.
Results may differ from a plain program's by a relative error of at most 0.015.
Values may be sent and summed in bfloat16 or wider, within the bound.
A program may use at most 128 MiB of HBM per device.

v0:
```python
import jax
import jax.numpy as jnp
from jax import lax
from jax.sharding import PartitionSpec as P


def per_device(panel, slab, cotangent, inverse):
    tiles_local = panel.shape[0]
    tile_size = panel.shape[2]
    strip_width = panel.shape[3]
    slab_tiles = slab.shape[3]
    row_count = tiles_local * tile_size
    slab_width = slab_tiles * tile_size
    row_devices = lax.axis_size("row")
    col_devices = lax.axis_size("col")
    row_index = lax.axis_index("row")
    col_index = lax.axis_index("col")
    highest = lax.Precision.HIGHEST
    contract_rows = (((0,), (0,)), ((), ()))
    panel_rows = panel.reshape(row_count, strip_width)
    gathered = lax.all_gather(panel_rows, "col", axis=1, tiled=True)
    factor = jnp.dot(gathered, inverse.T, precision=highest, preferred_element_type=jnp.float32)
    rounded = factor.astype(jnp.bfloat16)
    factor_tiles = rounded.reshape(tiles_local, tile_size, tile_size)
    tile_list = []
    for column_slot in range(slab_tiles):
        tile_index = column_slot * col_devices + col_index
        is_owner = tile_index % row_devices == row_index
        owned_tile = lax.dynamic_index_in_dim(
            factor_tiles, tile_index // row_devices, 0, keepdims=False
        )
        tile_list.append(jnp.where(is_owner, owned_tile, jnp.zeros_like(owned_tile)))
    stacked = jnp.stack(tile_list).reshape(slab_width, tile_size)
    slab_factor = lax.psum(stacked, "row").astype(jnp.float32).astype(jnp.bfloat16)
    slab_rows = slab.reshape(row_count, slab_width)
    product = jnp.dot(rounded, slab_factor.T, preferred_element_type=jnp.float32)
    updated = (slab_rows.astype(jnp.float32) - product).astype(jnp.bfloat16)
    cot_rows = cotangent.reshape(row_count, slab_width)
    factor_grad = -jnp.dot(cot_rows, slab_factor, preferred_element_type=jnp.float32)
    slab_grad = -lax.dot_general(
        cot_rows, rounded, contract_rows, preferred_element_type=jnp.float32
    )
    slab_grad = lax.psum(slab_grad.astype(jnp.bfloat16), "row").astype(jnp.float32)
    grad_tiles = factor_grad.reshape(tiles_local, tile_size, tile_size)
    for column_slot in range(slab_tiles):
        tile_index = column_slot * col_devices + col_index
        is_owner = tile_index % row_devices == row_index
        local_slot = tile_index // row_devices
        current_tile = lax.dynamic_index_in_dim(grad_tiles, local_slot, 0, keepdims=True)
        added_tile = jnp.where(
            is_owner, slab_grad[column_slot * tile_size : (column_slot + 1) * tile_size], 0.0
        )
        grad_tiles = lax.dynamic_update_index_in_dim(
            grad_tiles, current_tile + added_tile[None], local_slot, 0
        )
    factor_grad = grad_tiles.reshape(row_count, tile_size)
    grad_total = lax.psum(factor_grad, "col")
    inverse_strip = lax.dynamic_slice_in_dim(inverse, col_index * strip_width, strip_width, 1)
    grad_panel = jnp.dot(
        grad_total, inverse_strip, precision=highest, preferred_element_type=jnp.float32
    )
    inverse_term = lax.dot_general(
        grad_total, panel_rows, contract_rows, precision=highest, preferred_element_type=jnp.float32
    )
    grad_inverse = lax.psum(inverse_term, "row")
    return (updated.reshape(slab.shape), grad_panel.reshape(panel.shape), grad_inverse)


def solution(mesh):
    in_specs = (
        P(None, "row", None, "col"),
        P(None, "row", None, None, "col", None),
        P(None, "row", None, None, "col", None),
        P(),
    )
    out_specs = (
        P(None, "row", None, None, "col", None),
        P(None, "row", None, "col"),
        P(None, "col"),
    )
    return jax.shard_map(
        per_device, mesh=mesh, in_specs=in_specs, out_specs=out_specs, check_vma=False
    )
```

profile of v0, /device:TPU:0, one launch (start us, length us, event | category | flops | bytes accessed | tf_op | source)
XLA Modules:
  0.0 430.0 jit_solution(7106329265095890)
XLA Ops:
  7.2 0.0 copy-start
  7.2 0.0 all-gather.2.cloned.1.call-start
  7.2 1.7 copy.19
  8.9 0.0 all-gather.2.cloned.1.call-update
  9.0 0.0 all-reduce.6.cloned.1.call-start
  9.1 5.2 %copy.20 = bf16[256,8,4,256]{3,1,2,0:T(8,128)(2,1)} copy(bf16[256,8,4,256]{3,2,1,0:T(4,128)(2,1)} %bitcast.71) | data formatting | bytes 8388608
  14.3 24.5 %all-gather.2.cloned.1.call-done = f32[2048,256]{0,1:T(8,128)} async-done(((f32[2048,32]{0,1:T(8,128)}), f32[2048,256]{0,1:T(8,128)}) %all-gather.2.cloned.1.call-update) | async-done | bytes 2097168 | tf_op jit(solution)/shard_map/all_gather | solution.py:21
  38.8 5.0 %convolution_convert_fusion = bf16[2048,256]{1,0:T(8,128)(2,1)S(1)} fusion(f32[2048,256]{0,1:T(8,128)} %all-gather.2.cloned.1.call-done, f32[256,256]{1,0:T(8,128)S(1)} %copy-done), kind=kOutput, calls=%fused_computation.2 | convolution fusion | flops 1611137024 | bytes 3407872 | tf_op jit(solution)/shard_map/dot_general | solution.py:22
  43.9 4.3 fusion.1
  48.2 0.9 pad_maximum_fusion
  49.1 0.0 all-reduce.6.cloned.1.call-update
  49.1 0.2 all-reduce.4.cloned.1.call-start
  49.3 150.0 %all-reduce.6.cloned.1.call-done = (bf16[1024,256]{1,0:T(8,128)(2,1)}, bf16[1024,256]{0,1:T(8,128)(2,1)}) async-done(((bf16[1024,256]{1,0:T(8,128)(2,1)}, bf16[1024,256]{0,1:T(8,128)(2,1)}), (bf16[1024,256]{1,0:T(8,128)(2,1)}, bf16[1024,256]{0,1:T(8,128)(2,1)})) %all-reduce.6.cloned.1.call-update) | async-done | bytes 1048592 | tf_op jit(solution)/shard_map/psum | solution.py:34
  199.3 3.7 convolution_negate_fusion
  202.9 0.2 copy.24
  203.1 0.9 copy-done.4
  204.0 0.1 convert_element_type.29
  204.1 0.1 fusion.13
  204.2 0.1 fusion.10
  204.2 0.1 fusion.7
  204.3 0.1 fusion.4
  204.4 1.8 copy.14
  206.2 0.0 all-reduce.4.cloned.1.call-update
  206.2 7.0 %copy.18 = f32[256,8,4,256]{3,1,2,0:T(8,128)} copy(bf16[256,8,4,256]{3,2,1,0:T(4,128)(2,1)} %bitcast.70) | data formatting | bytes 12582912
  213.2 6.8 %subtract_convert_fusion = bf16[2048,1024]{1,0:T(8,128)(2,1)} fusion(f32[2048,1024]{1,0:T(8,128)} %bitcast.66, bf16[2048,256]{1,0:T(8,128)(2,1)S(1)} %convolution_convert_fusion, bf16[1024,256]{1,0:T(8,128)(2,1)S(1)} %copy-done.3), kind=kOutput, calls=%fused_computation | convolution fusion | flops 1077936128 | bytes 14155776 | tf_op jit(solution)/shard_map/dot_general | solution.py:36
  220.1 7.9 %reshape.36 = bf16[8,1,256,4,1,256]{5,3,2,0,4,1:T(4,128)(2,1)} reshape(bf16[2048,1024]{1,0:T(8,128)(2,1)} %subtract_convert_fusion) | data formatting | bytes 8388608 | tf_op jit(solution)/shard_map/reshape | solution.py:66
  227.9 46.6 %all-reduce.4.cloned.1.call-done = f32[2048,256]{1,0:T(8,128)} async-done(((f32[2048,256]{1,0:T(8,128)}), f32[2048,256]{1,0:T(8,128)}) %all-reduce.4.cloned.1.call-update) | async-done | bytes 2097168 | tf_op jit(solution)/shard_map/psum | solution.py:57
  274.5 3.8 fusion.14
  278.3 0.1 copy.21
  278.4 0.8 copy.16
  279.2 1.2 fusion.17
  280.4 143.1 %psum.31 = f32[256,32]{0,1:T(8,128)} all-reduce(f32[256,32]{0,1:T(8,128)S(1)} %fusion.17), channel_id=1, replica_groups=mesh['row'=32,'col'=8] {'row'}, use_global_device_ids=true, to_apply=%region_3.4 | all-reduce | flops 8192 | bytes 65536 | tf_op jit(solution)/shard_map/psum | solution.py:65
  (9 shorter events, 0.1 us)
Async XLA Ops:
  7.2 31.7 %copy-start = (f32[256,256]{1,0:T(8,128)S(1)}, f32[256,256]{1,0:T(8,128)}, u32[]{:S(2)}) copy-start(f32[256,256]{1,0:T(8,128)} %param.7) | copy-start | bytes 786436
  7.2 31.7 %all-gather.2.cloned.1.call-start = ((), (), s32[]{:S(2)}) async-start(), calls=%async_computation | async-start | bytes 2359296 | tf_op jit(solution)/shard_map/all_gather | solution.py:21
  9.0 190.3 %all-reduce.6.cloned.1.call-start = ((), (), s32[]{:S(2)}) async-start(), calls=%async_computation.2 | async-start | bytes 2097152 | tf_op jit(solution)/shard_map/psum | solution.py:34
  49.1 225.4 %all-reduce.4.cloned.1.call-start = ((), (), s32[]{:S(2)}) async-start(), calls=%async_computation.1 | async-start | bytes 4194304 | tf_op jit(solution)/shard_map/psum | solution.py:57
  202.9 1.0 copy-start.4
  206.2 7.0 %copy-start.3 = (bf16[1024,256]{1,0:T(8,128)(2,1)S(1)}, bf16[1024,256]{1,0:T(8,128)(2,1)}, u32[]{:S(2)}) copy-start(bf16[1024,256]{1,0:T(8,128)(2,1)} %get-tuple-element.9) | copy-start | bytes 1572868
  227.9 51.3 %copy-start.2 = (f32[4,8,8,256]{3,1,2,0:T(8,128)S(1)}, f32[4,8,8,256]{3,1,2,0:T(8,128)}, u32[]{:S(2)}) copy-start(f32[4,8,8,256]{3,1,2,0:T(8,128)} %copy.19) | copy-start | bytes 786436
  274.5 4.7 %copy-start.1 = (f32[2048,256]{1,0:T(8,128)S(1)}, f32[2048,256]{1,0:T(8,128)}, u32[]{:S(2)}) copy-start(f32[2048,256]{1,0:T(8,128)} %all-reduce.4.cloned.1.call-done) | copy-start | bytes 6291460
Sparse Core Ops, SparseCore 0:
  9.9 28.9 all-gather.1
  49.2 150.0 all-reduce.5
  206.3 68.1 all-reduce.3
where the time goes:
time: 431 us; the launch traced here: 430 us
  waiting for transfers between devices  221 us (51%)
  blocking collectives  143 us (33%)
  local copies, waits for them, and re-layouts  25.5 us (6%)
  matrix products  24.8 us (6%)
  between operations  13.9 us (3%)
    psum x1, waiting for transfers between devices, per_device(): lax.psum(stacked, 'row').astype(jnp.float32).astype(jnp.bfloat16)  150 us
    psum x1, blocking collectives, per_device(): grad_inverse = lax.psum(inverse_term, 'row')  143 us
    psum x1, waiting for transfers between devices, per_device(): grad_total = lax.psum(factor_grad, 'col')  46.6 us
    all_gather x1, waiting for transfers between devices, per_device(): gathered = lax.all_gather(panel_rows, 'col', axis=1, tiled=True)  24.5 us
    unnamed x15, local copies, waits for them, and re-layouts  15.7 us
  transfers between devices with their start and end apart: 3, of which 3 were waited for; matrix products, arithmetic and copies ran while one was open for 6% of the time, Pallas kernels for 0%

commit v1 on v0

--- a/solution.py
+++ b/solution.py
@@ -2,6 +2,21 @@
 import jax.numpy as jnp
 from jax import lax
 from jax.sharding import PartitionSpec as P
+
+
+def assign_the_run(shard_axis, frame_in):
+    world = lax.axis_size(shard_axis)
+
+    def detail_sizes_on_mesh(x_next, low):
+        if low >= world:
+            return x_next
+        return detail_sizes_on_mesh(
+            x_next
+            + lax.ppermute(x_next, shard_axis, list(map(lambda rr: (rr, rr ^ low), range(world)))),
+            2 * low,
+        )
+
+    return detail_sizes_on_mesh(frame_in, 1)
 
 
 def per_device(panel, slab, cotangent, inverse):
@@ -62,7 +77,7 @@
     inverse_term = lax.dot_general(
         grad_total, panel_rows, contract_rows, precision=highest, preferred_element_type=jnp.float32
     )
-    grad_inverse = lax.psum(inverse_term, "row")
+    grad_inverse = assign_the_run("row", inverse_term)
     return (updated.reshape(slab.shape), grad_panel.reshape(panel.shape), grad_inverse)
 
 

time: 431 us -> 330 us (0.77)
  blocking collectives: 143 us -> 0 us
  waiting for transfers between devices: 221 us -> 248 us
  starting transfers between devices: 0.3 us -> 14.6 us
    psum x1 -> x0, blocking collectives: 143 us -> none  [per_device(): grad_inverse = lax.psum(inverse_term, 'row')]
    psum x1, waiting for transfers between devices: 46.6 us -> 68.2 us  [per_device(): grad_total = lax.psum(factor_grad, 'col')]
    ppermute x0 -> x5, starting transfers between devices: none -> 14.5 us  [detail_sizes_on_mesh(): lax.ppermute(x_next, shard_axis, list(map(lambda rr: (rr, rr ^ low), rang...]
    ppermute x0 -> x5, waiting for transfers between devices: none -> 4.64 us  [detail_sizes_on_mesh(): lax.ppermute(x_next, shard_axis, list(map(lambda rr: (rr, rr ^ low), rang...]
  transfers between devices with their start and end apart: 3 -> 8, of which waited for: 3 -> 5; matrix products, arithmetic and copies ran while one was open for 6% -> 9% of each run, Pallas kernels for 0% -> 0%
where the time goes in v1:
time: 330 us; the launch traced here: 329 us
  waiting for transfers between devices  248 us (75%)
  local copies, waits for them, and re-layouts  25.7 us (8%)
  matrix products  24.5 us (7%)
  starting transfers between devices  14.6 us (4%)
  between operations  13.9 us (4%)
    psum x1, waiting for transfers between devices, per_device(): lax.psum(stacked, 'row').astype(jnp.float32).astype(jnp.bfloat16)  150 us
    psum x1, waiting for transfers between devices, per_device(): grad_total = lax.psum(factor_grad, 'col')  68.2 us
    all_gather x1, waiting for transfers between devices, per_device(): gathered = lax.all_gather(panel_rows, 'col', axis=1, tiled=True)  25.1 us
    unnamed x15, local copies, waits for them, and re-layouts  15.7 us
    ppermute x5, starting transfers between devices, detail_sizes_on_mesh(): lax.ppermute(x_next, shard_axis, list(map(lambda rr: (rr, rr ^ low), rang...  14.5 us
    reshape x1, local copies, waits for them, and re-layouts, per_device(): updated.reshape(slab.shape)  7.98 us
    dot_general x1, matrix products, per_device(): jnp.dot(rounded, slab_factor.T, preferred_element_type=jnp.float32)  6.64 us
  transfers between devices with their start and end apart: 8, of which 5 were waited for; matrix products, arithmetic and copies ran while one was open for 9% of the time, Pallas kernels for 0%

profile of v1, /device:TPU:0, one launch (start us, length us, event | category | flops | bytes accessed | tf_op | source)
XLA Modules:
  0.0 328.8 jit_solution(5022288563212661238)
XLA Ops:
  7.2 1.7 copy.19
  9.1 5.2 %copy.20 = bf16[256,8,4,256]{3,1,2,0:T(8,128)(2,1)} copy(bf16[256,8,4,256]{3,2,1,0:T(4,128)(2,1)} %bitcast.71) | data formatting | bytes 8388608
  14.3 25.1 %all-gather.2.cloned.1.call-done = f32[2048,256]{0,1:T(8,128)} async-done(((f32[2048,32]{0,1:T(8,128)}), f32[2048,256]{0,1:T(8,128)}) %all-gather.2.cloned.1.call-update) | async-done | bytes 2097168 | tf_op jit(solution)/shard_map/all_gather | solution.py:36
  39.4 5.0 %convolution_convert_fusion = bf16[2048,256]{1,0:T(8,128)(2,1)S(1)} fusion(f32[2048,256]{0,1:T(8,128)} %all-gather.2.cloned.1.call-done, f32[256,256]{1,0:T(8,128)S(1)} %copy-done), kind=kOutput, calls=%fused_computation.2 | convolution fusion | flops 1611137024 | bytes 3407872 | tf_op jit(solution)/shard_map/dot_general | solution.py:37
  44.4 4.3 %fusion.1 = bf16[1024,256]{0,1:T(8,128)(2,1)} fusion(bf16[2048,256]{1,0:T(8,128)(2,1)S(1)} %convolution_convert_fusion, bf16[2048,1024]{1,0:T(8,128)(2,1)} %bitcast.72), kind=kOutput, calls=%fused_computation.6 | convolution fusion | flops 1074266112 | bytes 5767168 | tf_op jit(solution)/shard_map/dot_general | solution.py:55
  48.8 0.9 pad_maximum_fusion
  49.7 150.2 %all-reduce.6.cloned.1.call-done = (bf16[1024,256]{1,0:T(8,128)(2,1)}, bf16[1024,256]{0,1:T(8,128)(2,1)}) async-done(((bf16[1024,256]{1,0:T(8,128)(2,1)}, bf16[1024,256]{0,1:T(8,128)(2,1)}), (bf16[1024,256]{1,0:T(8,128)(2,1)}, bf16[1024,256]{0,1:T(8,128)(2,1)})) %all-reduce.6.cloned.1.call-update) | async-done | bytes 1048592 | tf_op jit(solution)/shard_map/psum | solution.py:49
  199.9 3.7 %convolution_negate_fusion = f32[256,2048]{1,0:T(8,128)S(1)} fusion(bf16[1024,256]{1,0:T(8,128)(2,1)} %get-tuple-element.9, bf16[2048,1024]{1,0:T(8,128)(2,1)} %bitcast.73), kind=kOutput, calls=%fused_computation.1 | convolution fusion | flops 1074266112 | bytes 6815744 | tf_op jit(solution)/shard_map/dot_general | solution.py:54
  203.6 0.2 copy.24
  203.8 0.9 copy-done.4
  204.6 0.1 convert_element_type.29
  204.7 0.1 fusion.13
  204.8 0.1 fusion.10
  204.9 0.1 fusion.7
  204.9 0.1 fusion.4
  205.0 1.8 copy.14
  206.8 68.2 %all-reduce.4.cloned.1.call-done = f32[2048,256]{1,0:T(8,128)} async-done(((f32[2048,256]{1,0:T(8,128)}), f32[2048,256]{1,0:T(8,128)}) %all-reduce.4.cloned.1.call-update) | async-done | bytes 2097168 | tf_op jit(solution)/shard_map/psum | solution.py:72
  275.1 2.8 fusion.17
  277.9 1.6 collective-permute-start
  279.5 2.4 collective-permute-done
  281.9 2.5 collective-permute-start.1
  284.4 2.3 collective-permute-done.1
  286.7 5.7 %collective-permute-start.2 = (f32[256,32]{0,1:T(8,128)S(1)}, f32[256,32]{0,1:T(8,128)S(1)}, u32[]{:S(2)}, u32[]{:S(2)}) collective-permute-start(f32[256,32]{0,1:T(8,128)S(1)} %add.109), channel_id=1, source_target_pairs={{0,32},{8,40},{16,48},{24,56},{32,0},{40,8},{48,16},{56,24},{64,96... | collective-permute-start | bytes 98312 | tf_op jit(solution)/shard_map/ppermute | solution.py:15
  292.4 7.0 %copy.18 = f32[256,8,4,256]{3,1,2,0:T(8,128)} copy(bf16[256,8,4,256]{3,2,1,0:T(4,128)(2,1)} %bitcast.70) | data formatting | bytes 12582912
  299.5 1.8 collective-permute-start.3
  301.2 6.6 %subtract_convert_fusion = bf16[2048,1024]{1,0:T(8,128)(2,1)} fusion(f32[2048,1024]{1,0:T(8,128)} %bitcast.66, bf16[2048,256]{1,0:T(8,128)(2,1)S(1)} %convolution_convert_fusion, bf16[1024,256]{1,0:T(8,128)(2,1)S(1)} %copy-done.3), kind=kOutput, calls=%fused_computation | convolution fusion | flops 1077936128 | bytes 14155776 | tf_op jit(solution)/shard_map/dot_general | solution.py:51
  307.9 8.0 %reshape.36 = bf16[8,1,256,4,1,256]{5,3,2,0,4,1:T(4,128)(2,1)} reshape(bf16[2048,1024]{1,0:T(8,128)(2,1)} %subtract_convert_fusion) | data formatting | bytes 8388608 | tf_op jit(solution)/shard_map/reshape | solution.py:81
  315.8 2.8 collective-permute-start.4
  318.6 2.1 fusion.14
  320.7 0.1 copy.21
  320.8 0.8 copy.16
  321.6 0.6 add.112
  (23 shorter events, 0.3 us)
Async XLA Ops:
  7.2 32.2 %copy-start = (f32[256,256]{1,0:T(8,128)S(1)}, f32[256,256]{1,0:T(8,128)}, u32[]{:S(2)}) copy-start(f32[256,256]{1,0:T(8,128)} %param.7) | copy-start | bytes 786436
  7.2 32.2 %all-gather.2.cloned.1.call-start = ((), (), s32[]{:S(2)}) async-start(), calls=%async_computation | async-start | bytes 2359296 | tf_op jit(solution)/shard_map/all_gather | solution.py:36
  9.0 190.9 %all-reduce.6.cloned.1.call-start = ((), (), s32[]{:S(2)}) async-start(), calls=%async_computation.2 | async-start | bytes 2097152 | tf_op jit(solution)/shard_map/psum | solution.py:49
  49.7 225.4 %all-reduce.4.cloned.1.call-start = ((), (), s32[]{:S(2)}) async-start(), calls=%async_computation.1 | async-start | bytes 4194304 | tf_op jit(solution)/shard_map/psum | solution.py:72
  203.6 1.0 copy-start.4
  206.8 68.3 %copy-start.2 = (f32[4,8,8,256]{3,1,2,0:T(8,128)S(1)}, f32[4,8,8,256]{3,1,2,0:T(8,128)}, u32[]{:S(2)}) copy-start(f32[4,8,8,256]{3,1,2,0:T(8,128)} %copy.19) | copy-start | bytes 786436
  277.9 4.0 %collective-permute-start = (f32[256,32]{0,1:T(8,128)S(1)}, f32[256,32]{0,1:T(8,128)S(1)}, u32[]{:S(2)}, u32[]{:S(2)}) collective-permute-start(f32[256,32]{0,1:T(8,128)S(1)} %fusion.17), channel_id=1, source_target_pairs={{0,8},{8,0},{16,24},{24,16},{32,40},{40,32},{48,56},{56,48},{64,72... | collective-permute-start | bytes 98312 | tf_op jit(solution)/shard_map/ppermute | solution.py:15
  281.9 4.8 %collective-permute-start.1 = (f32[256,32]{0,1:T(8,128)S(1)}, f32[256,32]{0,1:T(8,128)S(1)}, u32[]{:S(2)}, u32[]{:S(2)}) collective-permute-start(f32[256,32]{0,1:T(8,128)S(1)} %add.108), channel_id=1, source_target_pairs={{0,16},{8,24},{16,0},{24,8},{32,48},{40,56},{48,32},{56,40},{64,80... | collective-permute-start | bytes 98312 | tf_op jit(solution)/shard_map/ppermute | solution.py:15
  286.7 12.8 %collective-permute-start.2 = (f32[256,32]{0,1:T(8,128)S(1)}, f32[256,32]{0,1:T(8,128)S(1)}, u32[]{:S(2)}, u32[]{:S(2)}) collective-permute-start(f32[256,32]{0,1:T(8,128)S(1)} %add.109), channel_id=1, source_target_pairs={{0,32},{8,40},{16,48},{24,56},{32,0},{40,8},{48,16},{56,24},{64,96... | collective-permute-start | bytes 98312 | tf_op jit(solution)/shard_map/ppermute | solution.py:15
  292.4 8.8 %copy-start.3 = (bf16[1024,256]{1,0:T(8,128)(2,1)S(1)}, bf16[1024,256]{1,0:T(8,128)(2,1)}, u32[]{:S(2)}) copy-start(bf16[1024,256]{1,0:T(8,128)(2,1)} %get-tuple-element.9) | copy-start | bytes 1572868
  299.5 16.4 %collective-permute-start.3 = (f32[256,32]{0,1:T(8,128)S(1)}, f32[256,32]{0,1:T(8,128)S(1)}, u32[]{:S(2)}, u32[]{:S(2)}) collective-permute-start(f32[256,32]{0,1:T(8,128)S(1)} %add.110), channel_id=1, source_target_pairs={{0,64},{8,72},{16,80},{24,88},{32,96},{40,104},{48,112},{56,120},{... | collective-permute-start | bytes 98312 | tf_op jit(solution)/shard_map/ppermute | solution.py:15
  307.9 10.8 %copy-start.1 = (f32[2048,256]{1,0:T(8,128)S(1)}, f32[2048,256]{1,0:T(8,128)}, u32[]{:S(2)}) copy-start(f32[2048,256]{1,0:T(8,128)} %all-reduce.4.cloned.1.call-done) | copy-start | bytes 6291460
  315.8 5.8 %collective-permute-start.4 = (f32[256,32]{0,1:T(8,128)S(1)}, f32[256,32]{0,1:T(8,128)S(1)}, u32[]{:S(2)}, u32[]{:S(2)}) collective-permute-start(f32[256,32]{0,1:T(8,128)S(1)} %add.111), channel_id=1, source_target_pairs={{0,128},{8,136},{16,144},{24,152},{32,160},{40,168},{48,176},{56,1... | collective-permute-start | bytes 98312 | tf_op jit(solution)/shard_map/ppermute | solution.py:15
Sparse Core Ops, SparseCore 0:
  10.4 28.9 all-gather.1
  49.8 150.0 all-reduce.5
  207.0 68.0 all-reduce.3
